TPU v7x, 512 devices: a whole 4x4x16 slice. The times are simulated.
512 devices in a mesh: dp: 8 (over x, core), expert: 64 (over z, y).
Axes of the slice: x: 4, y: 4, z: 16, core: 2. Of those that a mesh axis runs over, the one named last changes fastest.
Arguments:
- scores: int32 [64, 4096], P('expert', 'dp'), may hold values from 0 to 4095
- tokens: bfloat16 [4096, 4096], P('dp', 'expert'), may hold values from -6 to 6
- w_gate: bfloat16 [64, 1536, 4096], P('expert', 'dp'), may hold values from -0.09375 to 0.09375
- w_up: bfloat16 [64, 1536, 4096], P('expert', 'dp'), may hold values from -0.09375 to 0.09375
- w_down: bfloat16 [64, 1536, 4096], P('expert', 'dp'), may hold values from -0.15625 to 0.15625
Outputs:
- mixed: bfloat16 [4096, 4096], P('dp', 'expert')
Inputs may be any that keep to these rules, and one draw needn't show every extreme that they name: `scores`: score bins.
All inputs are finite; a program needn't handle non-finite values.
Results may differ from a plain program's by a relative error of at most 0.02.
Values may be sent and summed in bfloat16 or wider, within the bound.
A program may use at most 64 MiB of HBM per device.

v0:
```python
import jax
import jax.numpy as jnp
from jax import lax
from jax.sharding import PartitionSpec as P

CHOSEN = 4
LEVELS = 64


score_step = 1.0 / 512.0


def entering(value, axis, combine, identity):
    size, position = (lax.axis_size(axis), lax.axis_index(axis))
    everything = jax.tree.map(lambda part: lax.all_gather(part, axis), value)
    start = jax.tree.map(
        lambda part, zero: jnp.broadcast_to(jnp.asarray(zero, part.dtype), part.shape),
        value,
        identity,
    )

    def turn(k, before):
        reached = k < position
        new = combine(before, jax.tree.map(lambda part: part[k], everything))
        return jax.tree.map(lambda a, b: jnp.where(reached, a, b), new, before)

    return lax.fori_loop(0, size, turn, start)


def add_pair(earlier, later):
    return (earlier[0] + later[0], earlier[1] + later[1])


def project_rows(inputs, weight_rows):
    return lax.dot_general(
        inputs, weight_rows, (((1,), (1,)), ((), ())), preferred_element_type=jnp.float32
    )


def local(scores, tokens, w_gate, w_up, w_down):
    score_row = scores[0]
    tok_rows = score_row.shape[0]
    dp_size = lax.axis_size("dp")
    exp_size = lax.axis_size("expert")
    capacity = CHOSEN * tok_rows * dp_size // exp_size
    all_tokens = tok_rows * dp_size
    block = tokens.shape[1]
    first_tok = lax.axis_index("dp") * tok_rows
    bin_ids = jnp.arange(LEVELS, dtype=jnp.int32)
    coarse = score_row // LEVELS
    fine_bin = score_row % LEVELS
    local_coarse = jnp.sum(
        (coarse[:, None] == bin_ids[None, :]).astype(jnp.int32), axis=0, dtype=jnp.int32
    )
    coarse_counts = lax.psum(local_coarse, "dp")
    above_coarse = all_tokens - jnp.cumsum(coarse_counts, dtype=jnp.int32)
    cut_coarse = jnp.sum((above_coarse >= capacity).astype(jnp.int32), dtype=jnp.int32)
    need = capacity - jnp.sum(jnp.where(bin_ids == cut_coarse, above_coarse, 0), dtype=jnp.int32)
    inside = (coarse == cut_coarse)[:, None]
    local_fine = jnp.sum(
        ((fine_bin[:, None] == bin_ids[None, :]) & inside).astype(jnp.int32),
        axis=0,
        dtype=jnp.int32,
    )
    fine_counts = lax.psum(local_fine, "dp")
    above_fine = jnp.sum(fine_counts, dtype=jnp.int32) - jnp.cumsum(fine_counts, dtype=jnp.int32)
    cut_fine = jnp.sum((above_fine >= need).astype(jnp.int32), dtype=jnp.int32)
    allowed = need - jnp.sum(jnp.where(bin_ids == cut_fine, above_fine, 0), dtype=jnp.int32)
    cutoff = cut_coarse * LEVELS + cut_fine
    tie_mask = (score_row == cutoff).astype(jnp.int32)
    over_mask = (score_row > cutoff).astype(jnp.int32)
    tie_before, over_before = entering(
        (jnp.sum(tie_mask, dtype=jnp.int32), jnp.sum(over_mask, dtype=jnp.int32)),
        "dp",
        add_pair,
        (jnp.int32(0), jnp.int32(0)),
    )
    tie_rank = tie_before + jnp.cumsum(tie_mask, dtype=jnp.int32) - tie_mask
    chosen = (over_mask > 0) | (tie_mask > 0) & (tie_rank < allowed)
    chosen_int = chosen.astype(jnp.int32)
    slot_ids = (
        over_before
        + jnp.minimum(tie_before, allowed)
        + jnp.cumsum(chosen_int, dtype=jnp.int32)
        - chosen_int
    )
    weight = jnp.exp(score_row.astype(jnp.float32) * score_step)
    slot_dest = jnp.where(chosen, slot_ids, capacity)
    token_ids = (first_tok + jnp.arange(tok_rows, dtype=jnp.int32)).astype(jnp.float32)
    own_tables = jnp.zeros((2, capacity), jnp.float32)
    own_tables = own_tables.at[0, slot_dest].set(token_ids, mode="drop")
    own_tables = own_tables.at[1, slot_dest].set(weight, mode="drop")
    column = lax.psum(own_tables, "dp")
    table_data = lax.all_gather(column[None], "expert", axis=0, tiled=True)
    slot_tokens = table_data[:, 0, :].astype(jnp.int32)
    slot_weight = table_data[:, 1, :]
    gathered = lax.all_gather(tokens, "dp", axis=0, tiled=True)
    outgoing = gathered[slot_tokens]
    inputs = lax.all_to_all(outgoing, "expert", split_axis=0, concat_axis=2, tiled=True)[0]
    gate_val = project_rows(inputs, w_gate[0])
    up_val = project_rows(inputs, w_up[0])
    hidden = (jax.nn.silu(gate_val) * up_val).astype(jnp.bfloat16)
    computed = jnp.dot(hidden, w_down[0], preferred_element_type=jnp.float32).astype(jnp.bfloat16)[
        None
    ]
    returned = lax.all_to_all(computed, "expert", split_axis=2, concat_axis=0, tiled=True)
    term_rows = (
        jnp.zeros((all_tokens, block), jnp.float32)
        .at[slot_tokens.reshape(-1)]
        .add((returned.astype(jnp.float32) * slot_weight[:, :, None]).reshape(-1, block))
    )
    summed = lax.psum_scatter(
        term_rows.astype(jnp.bfloat16), "dp", scatter_dimension=0, tiled=True
    ).astype(jnp.float32)
    den_row = lax.psum(jnp.where(chosen, weight, jnp.float32(0.0)), "expert")
    return (summed / jnp.maximum(den_row, jnp.float32(1.0))[:, None]).astype(jnp.bfloat16)


def solution(mesh):
    in_specs = (
        P("expert", "dp"),
        P("dp", "expert"),
        P("expert", "dp", None),
        P("expert", "dp", None),
        P("expert", "dp", None),
    )
    out_specs = P("dp", "expert")
    return jax.shard_map(local, mesh=mesh, in_specs=in_specs, out_specs=out_specs, check_vma=False)
```

profile of v0, /device:TPU:8, one launch (start us, length us, event | category | flops | bytes accessed | tf_op | source)
XLA Modules:
  0.0 840.0 jit_solution(11131477647967400313)
XLA Ops:
  7.5 9.2 %psum.28 = s32[64,1]{0,1:T(1,128)S(1)} all-reduce(s32[64,1]{0,1:T(1,128)S(1)} %bitcast.111), channel_id=1, replica_groups=mesh['dp'=8,'expert'=64] {'dp'}, use_global_device_ids=true, to_apply=%region_1.2 | all-reduce | flops 64 | bytes 512 | tf_op jit(solution)/shard_map/psum | solution.py:55
  17.7 1.3 fusion.32
  20.5 7.3 psum.29
  30.8 1.4 fusion.34
  32.9 1.4 convert_reduce_fusion.3
  36.2 1.3 dynamic-update-slice.1
  37.5 1.3 dynamic-update-slice
  39.4 8.9 %all-reduce.4 = (s32[8]{0:T(128)S(1)}, s32[8]{0:T(128)S(1)}) all-reduce(s32[8]{0:T(128)S(1)} %dynamic-update-slice, s32[8]{0:T(128)S(1)} %dynamic-update-slice.1), channel_id=1, replica_groups=mesh['dp'=8,'expert'=64] {'dp'}, use_global_device_ids=true, to_apply=%add.2 | all-reduce | flops 16 | bytes 128
  48.3 20.9 %while.15 = (s32[]{:T(128)}, s32[]{:T(128)}, s32[]{:T(128)}, s32[]{:T(128)}, s32[8]{0:T(128)S(1)}, /*index=5*/s32[8]{0:T(128)S(1)}, s32[]{:T(128)}) while((s32[]{:T(128)}, s32[]{:T(128)}, s32[]{:T(128)}, s32[]{:T(128)}, s32[8]{0:T(128)S(1)}, /*index=5*/s32[8]{0:T(128)S(1)}, s32[]{:T(128)}) %tuple.38), condition=%wide.region_13.14_spmd, body=%wide.region_12.13_spmd.sunk | while | flops 7 | bytes 168 | solution.py:27
  71.8 24.8 %scatter_fusion = f32[2,256]{1,0:T(2,128)S(1)} fusion(f32[2,256]{1,0:T(2,128)S(1)} %broadcast_in_dim.38, s32[512]{0:T(512)S(1)} %bitcast.91, f32[512]{0:T(512)S(1)} %add_convert_fusion), kind=kCustom, calls=%fused_computation.1 | custom fusion | bytes 10240 | tf_op jit(solution)/shard_map/scatter | solution.py:91
  96.6 24.8 %scatter_fusion.1 = f32[2,256]{1,0:T(2,128)S(1)} fusion(f32[2,256]{1,0:T(2,128)S(1)} %scatter_fusion, s32[512]{0:T(512)S(1)} %bitcast.90, f32[512]{0:T(512)S(1)} %get-tuple-element.141), kind=kCustom, calls=%fused_computation.2 | custom fusion | bytes 10240 | tf_op jit(solution)/shard_map/scatter | solution.py:92
  121.4 12.4 %psum.30 = f32[1,2,256]{2,1,0:T(2,128)S(1)} all-reduce(f32[1,2,256]{2,1,0:T(2,128)S(1)} %bitcast.89), channel_id=1, replica_groups=mesh['dp'=8,'expert'=64] {'dp'}, use_global_device_ids=true, to_apply=%region_21.22 | all-reduce | flops 512 | bytes 4096 | tf_op jit(solution)/shard_map/psum | solution.py:93
  133.8 106.2 %all_gather.22 = f32[64,2,256]{2,1,0:T(2,128)S(1)} all-gather(f32[1,2,256]{2,1,0:T(2,128)S(1)} %psum.30), channel_id=1, replica_groups=mesh['dp'=8,'expert'=64] {'expert'}, dimensions={0}, use_global_device_ids=true | all-gather | bytes 133120 | tf_op jit(solution)/shard_map/all_gather | solution.py:94
  240.2 13.9 %all_gather.23 = bf16[4096,64]{1,0:T(8,128)(2,1)S(1)} all-gather(bf16[512,64]{1,0:T(8,128)(2,1)S(1)} %copy.44), channel_id=1, replica_groups=mesh['dp'=8,'expert'=64] {'dp'}, dimensions={0}, use_global_device_ids=true | all-gather | bytes 589824 | tf_op jit(solution)/shard_map/all_gather | solution.py:97
  254.1 57.4 %gather_fusion = bf16[16384,64]{1,0:T(8,128)(2,1)} fusion(bf16[4096,64]{1,0:T(8,128)(2,1)S(1)} %all_gather.23, s32[16384]{0:T(1024)S(1)} %broadcast_clamp_fusion), kind=kCustom, calls=%fused_computation | custom fusion | bytes 4259840 | tf_op jit(solution)/shard_map/gather | solution.py:98
  311.5 4.8 copy.45
  316.3 111.0 %all_to_all.24 = bf16[64,256,64]{1,2,0:T(8,128)(2,1)S(1)} all-to-all(bf16[64,256,64]{1,2,0:T(8,128)(2,1)} %copy.45), channel_id=1, replica_groups=mesh['dp'=8,'expert'=64] {'expert'}, dimensions={0} | all-to-all | bytes 4194304 | tf_op jit(solution)/shard_map/all_to_all | solution.py:99
  427.3 1.3 copy-done.1
  430.1 5.0 fusion
  435.1 10.0 %copy.46 = bf16[1,256,4096]{1,0,2:T(2,128)(2,1)} copy(bf16[1,256,4096]{2,1,0:T(8,128)(2,1)} %fusion) | data formatting | bytes 4194304 | tf_op jit(solution)/shard_map/broadcast_in_dim | solution.py:103
  445.6 22.9 %reduce.10 = bf16[4096,256]{1,0:T(8,128)(2,1)} reduce(bf16[4096,1,256]{2,1,0:T(2,128)(2,1)} %bitcast.95, bf16[]{:T(256)} %broadcast.348), dimensions={1}, to_apply=%bitcast.74.reduce_sub_computation | reduce | bytes 4194306
  468.5 4.0 reshape.377
  472.5 6.1 all-to-all-start.1
  478.8 99.3 %all-to-all-done.1 = bf16[64,2,8192]{2,1,0:T(2,128)(2,1)} async-done(((bf16[64,2,8192]{2,1,0:T(2,128)(2,1)}), bf16[64,2,8192]{2,1,0:T(2,128)(2,1)}, u32[]{:S(2)}, u32[]{:S(2)}) %all-to-all-start.1) | async-done | bytes 2097184 | tf_op jit(solution)/shard_map/all_to_all | solution.py:106
  578.1 10.4 %reshape.378 = bf16[4096,1,256]{2,1,0:T(2,128)(2,1)} reshape(bf16[64,2,8192]{2,1,0:T(2,128)(2,1)} %all-to-all-done.1) | data formatting | bytes 4194304
  588.6 2.5 copy.47
  592.1 2.3 broadcast_multiply_fusion
  594.4 6.9 copy.49
  601.3 89.1 %scatter_custom_fusion.2 = f32[4096,64]{1,0:T(8,128)} fusion(s32[16384]{0:T(1024)S(1)} %bitcast.102, f32[16384,64]{1,0:T(8,128)} %copy.49, f32[]{:T(128)} %constant.75.clone.1), kind=kCustom, calls=%fused_computation.15 | custom fusion | flops 1048576 | bytes 1049088 | tf_op jit(solution)/shard_map/scatter-add | solution.py:110
  690.4 2.7 copy.50
  693.1 138.6 %psum.31 = f32[512]{0:T(512)S(1)} all-reduce(f32[512]{0:T(512)S(1)} %get-tuple-element.131), channel_id=1, replica_groups=mesh['dp'=8,'expert'=64] {'expert'}, use_global_device_ids=true, to_apply=%region_24.25 | all-reduce | flops 512 | bytes 4096 | tf_op jit(solution)/shard_map/psum | solution.py:115
  831.7 1.5 divide_convert_fusion
  (70 shorter events, 23.3 us)
Async XLA Ops:
  6.5 422.7 %copy-start = (bf16[1,192,4096]{2,1,0:T(8,128)(2,1)S(1)}, bf16[1,192,4096]{2,1,0:T(8,128)(2,1)}, u32[]{:S(2)}) copy-start(bf16[1,192,4096]{2,1,0:T(8,128)(2,1)} %param.11) | copy-start | bytes 4718596
  96.6 143.5 %copy-start.4 = (bf16[512,64]{0,1:T(8,128)(2,1)S(1)}, bf16[512,64]{0,1:T(8,128)(2,1)}, u32[]{:S(2)}) copy-start(bf16[512,64]{0,1:T(8,128)(2,1)} %param.8) | copy-start | bytes 196612
  316.3 112.4 %copy-start.2 = (bf16[1,192,4096]{2,1,0:T(8,128)(2,1)S(1)}, bf16[1,192,4096]{2,1,0:T(8,128)(2,1)}, u32[]{:S(2)}) copy-start(bf16[1,192,4096]{2,1,0:T(8,128)(2,1)} %param.9) | copy-start | bytes 4718596
  427.3 1.4 copy-start.1
  428.6 1.4 copy-start.3
  472.5 105.7 %all-to-all-start.1 = ((bf16[64,2,8192]{2,1,0:T(2,128)(2,1)}), bf16[64,2,8192]{2,1,0:T(2,128)(2,1)}, u32[]{:S(2)}, u32[]{:S(2)}) async-start(bf16[64,2,8192]{2,1,0:T(2,128)(2,1)} %reshape.377), calls=%async_computation.1 | async-start | bytes 4194304 | tf_op jit(solution)/shard_map/all_to_all | solution.py:106
  478.6 353.1 %reduce-scatter.2.cloned.1.call-start = ((), (), s32[]{:S(2)}) async-start(), calls=%async_computation.3 | async-start | bytes 589824 | tf_op jit(solution)/shard_map/reduce_scatter | solution.py:112
Sparse Core Ops, SparseCore 0:
  693.2 28.9 reduce-scatter.1
where the time goes:
time: 842 us; the launch traced here: 840 us
  blocking collectives  407 us (48%)
  local copies, waits for them, and re-layouts  166 us (20%)
  other arithmetic  128 us (15%)
  waiting for transfers between devices  99.3 us (12%)
  between operations  16.3 us (2%)
  loops' own time  10.4 us (1%)
    psum x1, blocking collectives, local(): den_row = lax.psum(jnp.where(chosen, weight, jnp.float32(0.0)), 'expert')  139 us
    all_to_all x1, blocking collectives, local(): lax.all_to_all(outgoing, 'expert', split_axis=0, concat_axis=2, tiled=True)  111 us
    all_gather x1, blocking collectives, local(): table_data = lax.all_gather(column[None], 'expert', axis=0, tiled=True)  106 us
    all_to_all x1, waiting for transfers between devices, local(): lax.all_to_all(computed, 'expert', split_axis=2, concat_axis=0, tiled=True)  99.3 us
    scatter-add x1, other arithmetic, local(): term_rows = jnp.zeros((all_tokens, block), jnp.float32).at[slot_tokens.re...  89.1 us
    gather x2, local copies, waits for them, and re-layouts, local(): outgoing = gathered[slot_tokens]  62.2 us
    scatter x1, local copies, waits for them, and re-layouts, local(): own_tables = own_tables.at[0, slot_dest].set(token_ids, mode='drop')  24.8 us
    scatter x1, local copies, waits for them, and re-layouts, local(): own_tables = own_tables.at[1, slot_dest].set(weight, mode='drop')  24.8 us
  transfers between devices with their start and end apart: 2, of which 1 were waited for; matrix products, arithmetic and copies ran while one was open for 0% of the time, Pallas kernels for 0%

commit v1 on v0

v1 whole, which is shorter than its diff:
```python
import functools

import jax
import jax.numpy as jnp
from jax import lax
from jax.experimental import pallas as pl
from jax.experimental.pallas import tpu as pltpu
from jax.sharding import PartitionSpec as P

SCORE_BITS = 12
SCORE_STEP = 1.0 / 512.0
MESH = pl.DeviceIdType.MESH
VMEM = pl.BlockSpec(memory_space=pltpu.VMEM)


def params(collective_id):
    return pltpu.CompilerParams(
        collective_id=collective_id, has_side_effects=True, vmem_limit_bytes=48 * 1024 * 1024
    )


def greet(dp_size, exp_size, with_dp, with_expert):
    d, e = lax.axis_index("dp"), lax.axis_index("expert")
    barrier = pltpu.get_barrier_semaphore()
    count = 0
    if with_expert:

        @pl.loop(1, exp_size)
        def _(step):
            pl.semaphore_signal(
                barrier, inc=1, device_id=(d, lax.rem(e + step, exp_size)), device_id_type=MESH
            )

        count += exp_size - 1
    if with_dp:

        @pl.loop(1, dp_size)
        def _(step):
            pl.semaphore_signal(
                barrier, inc=1, device_id=(lax.rem(d + step, dp_size), e), device_id_type=MESH
            )

        count += dp_size - 1
    pl.semaphore_wait(barrier, count)


def select_kernel(capacity, tok_rows, d_ref, scores_ref, out_ref):
    d = d_ref[0]
    scores = scores_ref[...]
    rows, lanes = scores.shape
    cut = jnp.zeros((1, 1), jnp.int32)
    for bit in range(SCORE_BITS - 1, -1, -1):
        trial = cut + (1 << bit)
        count = jnp.sum((scores >= trial).astype(jnp.float32), keepdims=True)
        cut = jnp.where(count >= capacity, trial, cut)
    over = (scores > cut).astype(jnp.float32)
    tie = (scores == cut).astype(jnp.float32)
    allowed = capacity - jnp.sum(over, keepdims=True)
    lane_a = lax.broadcasted_iota(jnp.int32, (lanes, lanes), 0)
    lane_b = lax.broadcasted_iota(jnp.int32, (lanes, lanes), 1)
    before_lane = (lane_a < lane_b).astype(jnp.float32)
    row_a = lax.broadcasted_iota(jnp.int32, (rows, rows), 0)
    row_b = lax.broadcasted_iota(jnp.int32, (rows, rows), 1)
    before_row = (row_b < row_a).astype(jnp.float32)

    def rank(mask):
        in_row = jnp.dot(mask, before_lane, preferred_element_type=jnp.float32)
        totals = jnp.broadcast_to(jnp.sum(mask, axis=1, keepdims=True), (rows, lanes))
        return in_row + jnp.dot(before_row, totals, preferred_element_type=jnp.float32)

    chosen = jnp.maximum(over, jnp.where(rank(tie) < allowed, tie, 0.0))
    picked = chosen > 0.0
    slots = out_slots = capacity * tok_rows // (rows * lanes)
    slot_ids = jnp.where(picked, rank(chosen), -1.0).astype(jnp.int32) - d * slots
    place = lax.broadcasted_iota(jnp.int32, (slots, lanes), 0)
    lane = lax.broadcasted_iota(jnp.int32, (1, lanes), 1)
    kind = lax.broadcasted_iota(jnp.int32, (8, lanes), 0)
    table = jnp.zeros((8, slots), jnp.float32)
    for row in range(rows):
        hit = (slot_ids[row : row + 1, :] == place).astype(jnp.float32)
        score = scores[row : row + 1, :]
        entry = jnp.where(kind == 0, row, 0)
        entry = jnp.where(kind == 1, lane, entry)
        entry = jnp.where(kind == 2, score >> 6, entry)
        entry = jnp.where(kind == 3, score & 63, entry)
        table += lax.dot_general(
            entry.astype(jnp.float32),
            hit,
            (((1,), (1,)), ((), ())),
            preferred_element_type=jnp.float32,
        )
    table = table.astype(jnp.int32)
    per_row = tok_rows // lanes
    masked = jnp.where(picked, scores, -1)
    own = jnp.zeros((per_row, lanes), jnp.int32)
    for step in range(rows // per_row):
        own += jnp.where(d == step, masked[step * per_row : (step + 1) * per_row, :], 0)
    out_ref[...] = jnp.zeros_like(out_ref)
    out_ref[0:per_row, :] = own
    out_ref[per_row : per_row + 1, 0:slots] = table[0:1, :] * lanes + table[1:2, :]
    out_ref[per_row + 1 : per_row + 2, 0:slots] = table[2:3, :] * 64 + table[3:4, :]


def share_kernel(dp_size, exp_size, in_ref, out_ref, local_sem, send_sems, recv_sems):
    d, e = lax.axis_index("dp"), lax.axis_index("expert")
    greet(dp_size, exp_size, False, True)
    own = pltpu.make_async_copy(in_ref, out_ref.at[e], local_sem)
    own.start()

    def copy(step):
        peer = lax.rem(e + step, exp_size)
        return pltpu.make_async_remote_copy(
            src_ref=in_ref,
            dst_ref=out_ref.at[e],
            send_sem=send_sems.at[step],
            recv_sem=recv_sems.at[step],
            device_id=(d, peer),
            device_id_type=MESH,
        )

    @pl.loop(1, exp_size)
    def _(step):
        copy(step).start()

    own.wait()

    @pl.loop(1, exp_size)
    def _(step):
        copy(step).wait()


def swap_start(exp_size, src_ref, dst_ref, local_sem, send_sems, recv_sems):
    d, e = lax.axis_index("dp"), lax.axis_index("expert")
    own = pltpu.make_async_copy(src_ref.at[e], dst_ref.at[e], local_sem)
    own.start()

    def copy(step):
        peer = lax.rem(e + step, exp_size)
        return pltpu.make_async_remote_copy(
            src_ref=src_ref.at[peer],
            dst_ref=dst_ref.at[e],
            send_sem=send_sems.at[step],
            recv_sem=recv_sems.at[step],
            device_id=(d, peer),
            device_id_type=MESH,
        )

    @pl.loop(1, exp_size)
    def _(step):
        copy(step).start()

    own.wait()

    @pl.loop(1, exp_size)
    def _(step):
        copy(step).wait()


def dispatch_kernel(
    dp_size, exp_size, in_ref, out_ref, landed, x_own, local_sem, send_sems, recv_sems, dsend, drecv
):
    d, e = lax.axis_index("dp"), lax.axis_index("expert")
    chip, core = lax.div(d, 2), lax.rem(d, 2)
    chips = dp_size // 2
    greet(dp_size, exp_size, True, True)
    swap_start(exp_size, in_ref, landed, local_sem, send_sems, recv_sems)
    half = landed.shape[1]
    left = lax.broadcasted_iota(jnp.int32, (half, 128), 1) < 64
    for pair in range(exp_size // 2):
        a = landed[2 * pair].astype(jnp.float32)
        b = landed[2 * pair + 1].astype(jnp.float32)
        cols = pl.ds(pair * 128, 128)
        x_own[0:half, cols] = jnp.where(left, a, pltpu.roll(b, 64, 1)).astype(jnp.bfloat16)
        x_own[half : 2 * half, cols] = jnp.where(left, pltpu.roll(a, 64, 1), b).astype(jnp.bfloat16)
    own = pltpu.make_async_copy(x_own, out_ref.at[d], local_sem)
    own.start()

    def across(step):
        return pltpu.make_async_remote_copy(
            src_ref=x_own,
            dst_ref=out_ref.at[d],
            send_sem=dsend.at[step],
            recv_sem=drecv.at[step],
            device_id=(lax.rem(chip + step, chips) * 2 + core, e),
            device_id_type=MESH,
        )

    def beside(step):
        source = lax.rem(chip - step + chips, chips) * 2 + core
        return pltpu.make_async_remote_copy(
            src_ref=x_own if step == 0 else out_ref.at[source],
            dst_ref=out_ref.at[source],
            send_sem=dsend.at[chips + step],
            recv_sem=drecv.at[chips + step],
            device_id=(chip * 2 + 1 - core, e),
            device_id_type=MESH,
        )

    for step in range(1, chips):
        across(step).start()
    beside(0).start()
    for step in range(1, chips):
        across(step).wait_recv()
        beside(step).start()
    for step in range(1, chips):
        across(step).wait_send()
    for step in range(chips):
        beside(step).wait()
    own.wait()


def return_kernel(
    dp_size,
    exp_size,
    in_ref,
    out_ref,
    from_core,
    pair_sum,
    from_chip,
    packed,
    local_sem,
    send_sems,
    recv_sems,
    dsend,
    drecv,
):
    d, e = lax.axis_index("dp"), lax.axis_index("expert")
    chip, core = lax.div(d, 2), lax.rem(d, 2)
    chips = dp_size // 2
    greet(dp_size, exp_size, True, True)

    def beside(step):
        target = lax.rem(chip + step, chips)
        return pltpu.make_async_remote_copy(
            src_ref=in_ref.at[target * 2 + 1 - core],
            dst_ref=from_core.at[step],
            send_sem=dsend.at[chips + step],
            recv_sem=drecv.at[chips + step],
            device_id=(chip * 2 + 1 - core, e),
            device_id_type=MESH,
        )

    def across(step):
        return pltpu.make_async_remote_copy(
            src_ref=pair_sum.at[step],
            dst_ref=from_chip.at[step],
            send_sem=dsend.at[step],
            recv_sem=drecv.at[step],
            device_id=(lax.rem(chip + step, chips) * 2 + core, e),
            device_id_type=MESH,
        )

    order = [2, 1, 3, 0]
    for step in order:
        beside(step).start()
    for step in order[:-1]:
        beside(step).wait_recv()
        mine = in_ref[lax.rem(chip + step, chips) * 2 + core].astype(jnp.float32)
        pair_sum[step] = (mine + from_core[step].astype(jnp.float32)).astype(jnp.bfloat16)
        across(step).start()
    beside(0).wait_recv()
    for step in order[:-1]:
        across(step).wait_recv()
    half = packed.shape[1]
    left = lax.broadcasted_iota(jnp.int32, (half, 128), 1) < 64
    for pair in range(exp_size // 2):
        cols = pl.ds(pair * 128, 128)
        total = in_ref[d, :, cols].astype(jnp.float32) + from_core[0, :, cols].astype(jnp.float32)
        for step in range(1, chips):
            total += from_chip[step, :, cols].astype(jnp.float32)
        a, b = total[0:half], total[half : 2 * half]
        packed[2 * pair] = jnp.where(left, a, pltpu.roll(b, 64, 1)).astype(jnp.bfloat16)
        packed[2 * pair + 1] = jnp.where(left, pltpu.roll(a, 64, 1), b).astype(jnp.bfloat16)
    for step in order[:-1]:
        across(step).wait_send()
    for step in order:
        beside(step).wait_send()
    swap_start(exp_size, packed, out_ref, local_sem, send_sems, recv_sems)


def finish_kernel(dp_size, exp_size, in_ref, den_ref, out_ref, landed, send_sems, recv_sems):
    d, e = lax.axis_index("dp"), lax.axis_index("expert")
    greet(dp_size, exp_size, True, False)

    def copy(step):
        peer = lax.rem(d + step, dp_size)
        return pltpu.make_async_remote_copy(
            src_ref=in_ref.at[peer],
            dst_ref=landed.at[step],
            send_sem=send_sems.at[step],
            recv_sem=recv_sems.at[step],
            device_id=(peer, e),
            device_id_type=MESH,
        )

    for step in range(1, dp_size):
        copy(step).start()
    for step in range(1, dp_size):
        copy(step).wait()
    total = in_ref[d].astype(jnp.float32)
    for step in range(1, dp_size):
        total += landed[step].astype(jnp.float32)
    out_ref[...] = (total / den_ref[...]).astype(jnp.bfloat16)


def project_rows(inputs, weight_rows):
    return lax.dot_general(
        inputs, weight_rows, (((1,), (1,)), ((), ())), preferred_element_type=jnp.float32
    )


def local(capacity, dp_size, exp_size, scores, tokens, w_gate, w_up, w_down):
    tok_rows, block = tokens.shape
    all_tokens = tok_rows * dp_size
    width = block * exp_size
    slots = capacity // dp_size
    half = slots // 2
    dma = pltpu.SemaphoreType.DMA
    d = lax.axis_index("dp")
    all_scores = lax.all_gather(scores[0], "dp", axis=0, tiled=True).reshape(-1, 128)
    gathered = lax.all_gather(tokens, "dp", axis=0, tiled=True)
    block_out = pl.pallas_call(
        functools.partial(select_kernel, capacity, tok_rows),
        out_shape=jax.ShapeDtypeStruct((8, 128), jnp.int32),
        in_specs=[pl.BlockSpec(memory_space=pltpu.SMEM), VMEM],
        out_specs=VMEM,
    )(d.astype(jnp.int32).reshape(1), all_scores)
    tables = pl.pallas_call(
        functools.partial(share_kernel, dp_size, exp_size),
        out_shape=jax.ShapeDtypeStruct((exp_size, 8, 128), jnp.int32),
        in_specs=[VMEM],
        out_specs=VMEM,
        scratch_shapes=[dma, dma((exp_size,)), dma((exp_size,))],
        compiler_params=params(0),
    )(block_out)
    per_row = tok_rows // 128
    masked = tables[:, 0:per_row, :].reshape(exp_size, tok_rows)
    den = jnp.sum(jnp.where(masked >= 0, jnp.exp(masked.astype(jnp.float32) * SCORE_STEP), 0.0), axis=0)
    den = jnp.maximum(den, 1.0)
    slot_tokens = tables[:, per_row, 0:slots]
    slot_weight = jnp.exp(tables[:, per_row + 1, 0:slots].astype(jnp.float32) * SCORE_STEP)
    low, high = gathered[slot_tokens[:, :half]], gathered[slot_tokens[:, half:]]
    outgoing = jnp.concatenate([low, high], axis=-1)
    inputs = pl.pallas_call(
        functools.partial(dispatch_kernel, dp_size, exp_size),
        out_shape=jax.ShapeDtypeStruct((dp_size, slots, width), jnp.bfloat16),
        in_specs=[VMEM],
        out_specs=VMEM,
        scratch_shapes=[
            pltpu.VMEM((exp_size, half, 128), jnp.bfloat16),
            pltpu.VMEM((slots, width), jnp.bfloat16),
            dma,
            dma((exp_size,)),
            dma((exp_size,)),
            dma((dp_size,)),
            dma((dp_size,)),
        ],
        compiler_params=params(1),
    )(outgoing).reshape(capacity, width)
    gate_val = project_rows(inputs, w_gate[0])
    up_val = project_rows(inputs, w_up[0])
    hidden = (jax.nn.silu(gate_val) * up_val).astype(jnp.bfloat16)
    computed = jnp.dot(hidden, w_down[0], preferred_element_type=jnp.float32).astype(jnp.bfloat16)
    returned = pl.pallas_call(
        functools.partial(return_kernel, dp_size, exp_size),
        out_shape=jax.ShapeDtypeStruct((exp_size, half, 128), jnp.bfloat16),
        in_specs=[VMEM],
        out_specs=VMEM,
        scratch_shapes=[
            pltpu.VMEM((dp_size // 2, slots, width), jnp.bfloat16),
            pltpu.VMEM((dp_size // 2, slots, width), jnp.bfloat16),
            pltpu.VMEM((dp_size // 2, slots, width), jnp.bfloat16),
            pltpu.VMEM((exp_size, half, 128), jnp.bfloat16),
            dma,
            dma((exp_size,)),
            dma((exp_size,)),
            dma((dp_size,)),
            dma((dp_size,)),
        ],
        compiler_params=params(2),
    )(computed.reshape(dp_size, slots, width))
    values = jnp.concatenate([returned[:, :, :block], returned[:, :, block:]], axis=1)
    terms = values.astype(jnp.float32) * slot_weight[:, :, None]
    sums = (
        jnp.zeros((all_tokens, block), jnp.float32)
        .at[slot_tokens.reshape(-1)]
        .add(terms.reshape(-1, block))
    ).astype(jnp.bfloat16)
    sums = sums.reshape(dp_size, 2, tok_rows // 2, block)
    sums = jnp.concatenate([sums[:, 0], sums[:, 1]], axis=-1)
    den_pair = jnp.broadcast_to(den.reshape(2, tok_rows // 2, 1), (2, tok_rows // 2, block))
    den_pair = jnp.concatenate([den_pair[0], den_pair[1]], axis=-1)
    mixed = pl.pallas_call(
        functools.partial(finish_kernel, dp_size, exp_size),
        out_shape=jax.ShapeDtypeStruct((tok_rows // 2, 2 * block), jnp.bfloat16),
        in_specs=[VMEM, VMEM],
        out_specs=VMEM,
        scratch_shapes=[
            pltpu.VMEM((dp_size, tok_rows // 2, 2 * block), jnp.bfloat16),
            dma((dp_size,)),
            dma((dp_size,)),
        ],
        compiler_params=params(3),
    )(sums, den_pair)
    return jnp.concatenate([mixed[:, :block], mixed[:, block:]], axis=0)


def solution(mesh):
    dp_size, exp_size = mesh.shape["dp"], mesh.shape["expert"]
    in_specs = (
        P("expert", "dp"),
        P("dp", "expert"),
        P("expert", "dp", None),
        P("expert", "dp", None),
        P("expert", "dp", None),
    )

    def layer(scores, tokens, w_gate, w_up, w_down):
        capacity = 4 * scores.shape[1] // exp_size
        return jax.shard_map(
            functools.partial(local, capacity, dp_size, exp_size),
            mesh=mesh,
            in_specs=in_specs,
            out_specs=P("dp", "expert"),
            check_vma=False,
        )(scores, tokens, w_gate, w_up, w_down)

    return layer
```

time: 842 us -> 197 us (0.23)
  the two profiles are of different devices: /device:TPU:8 before, /device:TPU:1 now
where the time goes in v1:
time: 197 us
  Pallas kernels  123 us (62%)
  blocking collectives  35.8 us (18%)
  local copies, waits for them, and re-layouts  16.6 us (8%)
  other arithmetic  14.9 us (8%)
  matrix products  6.29 us (3%)
    pallas_call x1, Pallas kernels, local(): pl.pallas_call(functools.partial(dispatch_kernel, dp_size, exp_size), out...  43.1 us
    pallas_call x1, Pallas kernels, local(): pl.pallas_call(functools.partial(return_kernel, dp_size, exp_size), out_s...  39.3 us
    pallas_call x1, Pallas kernels, local(): pl.pallas_call(functools.partial(share_kernel, dp_size, exp_size), out_sh...  25.3 us
    all_gather x1, blocking collectives, local(): lax.all_gather(scores[0], 'dp', axis=0, tiled=True).reshape(-1, 128)  18.9 us
    all_gather x1, blocking collectives, local(): gathered = lax.all_gather(tokens, 'dp', axis=0, tiled=True)  16.8 us
    scatter-add x1, other arithmetic, local(): sums = jnp.zeros((all_tokens, block), jnp.float32).at[slot_tokens.reshape...  13.9 us
    pallas_call x1, Pallas kernels, local(): pl.pallas_call(functools.partial(finish_kernel, dp_size, exp_size), out_s...  11.7 us
    unnamed x15, local copies, waits for them, and re-layouts  5.62 us

profile of v1, /device:TPU:1, one launch (start us, length us, event | category | flops | bytes accessed | tf_op | source)
XLA Modules:
  0.0 196.7 jit_solution(8268990941844049222)
XLA Ops:
  0.0 18.9 %all-gather = s32[1,4096]{1,0:T(1,128)} all-gather(s32[1,512]{1,0:T(1,128)} %param.5), channel_id=2, replica_groups=mesh['dp'=8,'expert'=64] {'dp'}, dimensions={1}, use_global_device_ids=true | all-gather | bytes 18432 | tf_op jit(solution)/shard_map/all_gather | solution.py:320
  18.9 3.4 %shard_map.55.in_ref = s32[8,128]{1,0:T(8,128)} custom-call(s32[1]{0:T(128)} %bitcast.d_ref, s32[32,128]{1,0:T(8,128)} %bitcast.44), custom_call_target="tpu_custom_call" | custom-call | tf_op jit(solution)/shard_map/pallas_call | solution.py:322
  22.4 1.0 copy.18
  23.4 0.7 copy-done.3
  24.0 25.3 %shard_map.56 = s32[64,8,128]{2,1,0:T(8,128)S(1)} custom-call(s32[8,128]{1,0:T(8,128)S(1)} %copy-done.3), custom_call_target="tpu_custom_call" | custom-call | tf_op jit(solution)/shard_map/pallas_call | solution.py:328
  49.5 0.1 exponential_reduce_fusion
  49.6 0.1 fusion.25
  50.2 0.1 broadcast_in_dim.31
  50.3 0.1 broadcast_in_dim.33
  50.4 0.1 pad_maximum_fusion.3.den_ref
  50.5 16.8 %all_gather.7 = bf16[4096,64]{1,0:T(8,128)(2,1)S(1)} all-gather(bf16[512,64]{1,0:T(8,128)(2,1)S(1)} %copy.18), channel_id=1, replica_groups=mesh['dp'=8,'expert'=64] {'dp'}, dimensions={0}, use_global_device_ids=true | all-gather | bytes 589824 | tf_op jit(solution)/shard_map/all_gather | solution.py:321
  67.3 3.2 %gather_fusion.1 = bf16[1024,64]{1,0:T(8,128)(2,1)S(1)} fusion(bf16[4096,64]{1,0:T(8,128)(2,1)S(1)} %all_gather.7, s32[1024]{0:T(1024)S(1)} %broadcast_clamp_fusion), kind=kCustom, calls=%fused_computation.1 | custom fusion | bytes 266240 | tf_op jit(solution)/shard_map/gather | solution.py:342
  70.6 3.2 %gather_fusion = bf16[1024,64]{1,0:T(8,128)(2,1)S(1)} fusion(bf16[4096,64]{1,0:T(8,128)(2,1)S(1)} %all_gather.7, s32[1024]{0:T(1024)S(1)} %broadcast_clamp_fusion.1), kind=kCustom, calls=%fused_computation | custom fusion | bytes 266240 | tf_op jit(solution)/shard_map/gather | solution.py:342
  73.8 0.1 pad_maximum_fusion.2.in_ref
  73.9 43.1 %shard_map.57 = bf16[8,32,4096]{2,1,0:T(8,128)(2,1)S(1)} custom-call(bf16[64,16,128]{2,1,0:T(8,128)(2,1)S(1)} %pad_maximum_fusion.2.in_ref), custom_call_target="tpu_custom_call" | custom-call | tf_op jit(solution)/shard_map/pallas_call | solution.py:344
  117.0 1.3 copy-done.1
  118.3 0.8 fusion.3
  119.2 5.4 %convolution_convert_fusion = bf16[256,4096]{1,0:T(8,128)(2,1)} fusion(bf16[1,192,4096]{2,1,0:T(8,128)(2,1)S(1)} %copy-done, bf16[256,4096]{1,0:T(8,128)(2,1)} %bitcast.36, bf16[1,192,4096]{2,1,0:T(8,128)(2,1)S(1)} %copy-done.4, f32[256,192]{0,1:T(8,128)S(1)} %fusion.3), kind=kOutput, calls=%fused_computation.3 | convolution fusion | flops 806649856 | bytes 7536640 | tf_op jit(solution)/shard_map/dot_general | solution.py:363
  124.7 1.6 copy-done.2
  126.3 39.3 %shard_map.58 = bf16[64,16,128]{2,1,0:T(8,128)(2,1)S(1)} custom-call(bf16[8,32,4096]{2,1,0:T(8,128)(2,1)S(1)} %bitcast.37), custom_call_target="tpu_custom_call" | custom-call | tf_op jit(solution)/shard_map/pallas_call | solution.py:364
  165.6 0.1 fusion.24
  165.7 0.1 pad_maximum_fusion
  165.8 13.9 %scatter_custom_fusion = f32[4096,64]{1,0:T(8,128)} fusion(s32[2048]{0:T(1024)S(1)} %bitcast.45, bf16[2048,64]{1,0:T(8,128)(2,1)S(1)} %bitcast.40, f32[]{:T(128)} %constant.7.clone.1, f32[2048]{0:T(1024)S(1)} %exp.20), kind=kCustom, calls=%fused_computation.12 | custom fusion | flops 393216 | bytes 1581060 | tf_op jit(solution)/shard_map/scatter-add | solution.py:387
  179.7 1.9 copy.19
  181.7 0.4 reshape.90
  182.0 0.7 fusion.23
  182.8 0.5 copy.23
  183.3 0.5 copy.24
  183.8 0.3 pad_maximum_fusion.1.in_ref
  184.1 11.7 %shard_map.59 = bf16[256,128]{1,0:T(8,128)(2,1)S(1)} custom-call(bf16[8,256,128]{2,1,0:T(8,128)(2,1)S(1)} %pad_maximum_fusion.1.in_ref, f32[256,128]{1,0:T(8,128)S(1)} %pad_maximum_fusion.3.den_ref), custom_call_target="tpu_custom_call" | custom-call | tf_op jit(solution)/shard_map/pallas_call | solution.py:393
  195.9 0.1 fusion.26
  196.0 0.7 copy.22
  (21 shorter events, 0.6 us)
Async XLA Ops:
  0.0 119.2 %copy-start = (bf16[1,192,4096]{2,1,0:T(8,128)(2,1)S(1)}, bf16[1,192,4096]{2,1,0:T(8,128)(2,1)}, u32[]{:S(2)}) copy-start(bf16[1,192,4096]{2,1,0:T(8,128)(2,1)} %param.9) | copy-start | bytes 4718596
  23.4 0.7 copy-start.3
  73.8 44.6 %copy-start.5 = (bf16[1,192,4096]{2,1,0:T(8,128)(2,1)S(1)}, bf16[1,192,4096]{2,1,0:T(8,128)(2,1)}, u32[]{:S(2)}) copy-start(bf16[1,192,4096]{2,1,0:T(8,128)(2,1)} %param.7) | copy-start | bytes 4718596
  117.0 1.3 copy-start.1
  117.0 2.2 %copy-start.4 = (bf16[1,192,4096]{2,1,0:T(8,128)(2,1)S(1)}, bf16[1,192,4096]{2,1,0:T(8,128)(2,1)}, u32[]{:S(2)}) copy-start(bf16[1,192,4096]{2,1,0:T(8,128)(2,1)} %param.8) | copy-start | bytes 4718596
  124.7 1.6 copy-start.2

commit v2 on v1

v2 whole, which is shorter than its diff:
```python
import functools

import jax
import jax.numpy as jnp
from jax import lax
from jax.experimental import pallas as pl
from jax.experimental.pallas import tpu as pltpu
from jax.sharding import PartitionSpec as P

SCORE_BITS = 12
SCORE_STEP = 1.0 / 512.0
MESH = pl.DeviceIdType.MESH
VMEM = pl.BlockSpec(memory_space=pltpu.VMEM)


def params(collective_id):
    return pltpu.CompilerParams(
        collective_id=collective_id, has_side_effects=True, vmem_limit_bytes=56 * 1024 * 1024
    )


def hail(dp_size, exp_size):
    d, e = lax.axis_index("dp"), lax.axis_index("expert")
    barrier = pltpu.get_barrier_semaphore()

    @pl.loop(1, dp_size)
    def _(step):
        pl.semaphore_signal(
            barrier, inc=1, device_id=(lax.rem(d + step, dp_size), e), device_id_type=MESH
        )

    @pl.loop(1, exp_size)
    def _(step):
        pl.semaphore_signal(
            barrier, inc=1, device_id=(d, lax.rem(e + step, exp_size)), device_id_type=MESH
        )


def meet(dp_size, exp_size):
    pl.semaphore_wait(pltpu.get_barrier_semaphore(), dp_size + exp_size - 2)


def select(capacity, tok_rows, d, scores, table_ref):
    rows, lanes = scores.shape
    cut = jnp.zeros((1, 1), jnp.int32)
    for bit in range(SCORE_BITS - 1, -1, -1):
        trial = cut + (1 << bit)
        count = jnp.sum((scores >= trial).astype(jnp.float32), keepdims=True)
        cut = jnp.where(count >= capacity, trial, cut)
    over = (scores > cut).astype(jnp.float32)
    tie = (scores == cut).astype(jnp.float32)
    allowed = capacity - jnp.sum(over, keepdims=True)
    lane_a = lax.broadcasted_iota(jnp.int32, (lanes, lanes), 0)
    lane_b = lax.broadcasted_iota(jnp.int32, (lanes, lanes), 1)
    before_lane = (lane_a < lane_b).astype(jnp.float32)
    row_a = lax.broadcasted_iota(jnp.int32, (rows, rows), 0)
    row_b = lax.broadcasted_iota(jnp.int32, (rows, rows), 1)
    before_row = (row_b < row_a).astype(jnp.float32)

    def rank(mask):
        in_row = jnp.dot(mask, before_lane, preferred_element_type=jnp.float32)
        totals = jnp.broadcast_to(jnp.sum(mask, axis=1, keepdims=True), (rows, lanes))
        return in_row + jnp.dot(before_row, totals, preferred_element_type=jnp.float32)

    chosen = jnp.maximum(over, jnp.where(rank(tie) < allowed, tie, 0.0))
    slots = capacity * tok_rows // (rows * lanes)
    slot_ids = jnp.where(chosen > 0.0, rank(chosen), -1.0).astype(jnp.int32) - d * slots
    place = lax.broadcasted_iota(jnp.int32, (slots, lanes), 0)
    lane = lax.broadcasted_iota(jnp.int32, (1, lanes), 1)
    kind = lax.broadcasted_iota(jnp.int32, (8, lanes), 0)
    table = jnp.zeros((8, slots), jnp.float32)
    for row in range(rows):
        hit = (slot_ids[row : row + 1, :] == place).astype(jnp.float32)
        score = scores[row : row + 1, :]
        entry = jnp.where(kind == 0, row, 0)
        entry = jnp.where(kind == 1, lane, entry)
        entry = jnp.where(kind == 2, score >> 6, entry)
        entry = jnp.where(kind == 3, score & 63, entry)
        table += lax.dot_general(
            entry.astype(jnp.float32),
            hit,
            (((1,), (1,)), ((), ())),
            preferred_element_type=jnp.float32,
        )
    table = table.astype(jnp.int32)
    table_ref[...] = jnp.zeros_like(table_ref)
    table_ref[0:1, 0:slots] = table[0:1, :] * lanes + table[1:2, :]
    table_ref[1:2, 0:slots] = table[2:3, :] * 64 + table[3:4, :]


def turn_tables(exp_size, tables_ref, flat, turned):
    for expert in range(exp_size):
        flat[2 * expert : 2 * expert + 2, :] = tables_ref[expert].astype(jnp.float32)
    turned[...] = jnp.transpose(flat[...])


def spread(exp_size, slots, turned, token_of):
    for expert in range(exp_size):
        column = turned[0:slots, 2 * expert : 2 * expert + 1].astype(jnp.int32)
        token_of[expert * slots : (expert + 1) * slots, :] = jnp.broadcast_to(column, (slots, 128))


def one_hot(token_of, first, tok_rows):
    lane = lax.broadcasted_iota(jnp.int32, token_of.shape, 1)
    own = token_of[...] - first
    parts = [
        jnp.where(own == lane + step * 128, 1.0, 0.0).astype(jnp.bfloat16)
        for step in range(tok_rows // 128)
    ]
    return jnp.concatenate(parts, axis=1)


def expert_copy(exp_size, src_of, dst_ref, send_sems, recv_sems):
    d, e = lax.axis_index("dp"), lax.axis_index("expert")

    def copy(step):
        peer = lax.rem(e + step, exp_size)
        return pltpu.make_async_remote_copy(
            src_ref=src_of(peer),
            dst_ref=dst_ref.at[e],
            send_sem=send_sems.at[step],
            recv_sem=recv_sems.at[step],
            device_id=(d, peer),
            device_id_type=MESH,
        )

    return copy


def start_all(copy, size):
    @pl.loop(1, size)
    def _(step):
        copy(step).start()


def wait_all(copy, size):
    @pl.loop(1, size)
    def _(step):
        copy(step).wait()


def dispatch_kernel(
    capacity,
    dp_size,
    exp_size,
    scores_ref,
    tokens_ref,
    out_ref,
    tables_ref,
    scores_all,
    scores_flat,
    tokens_all,
    table_own,
    flat,
    turned,
    token_of,
    picked,
    packed,
    landed,
    x_own,
    ssend,
    srecv,
    tsend,
    trecv,
    send_sems,
    recv_sems,
    send_sems2,
    recv_sems2,
    dsend,
    drecv,
):
    d, e = lax.axis_index("dp"), lax.axis_index("expert")
    chip, core = lax.div(d, 2), lax.rem(d, 2)
    chips = dp_size // 2
    tok_rows = tokens_ref.shape[1]
    slots = capacity // dp_size
    hail(dp_size, exp_size)
    scores_all[d] = scores_ref[...]
    tokens_all[d] = tokens_ref[...]
    meet(dp_size, exp_size)

    def row_copy(src_ref, dst_ref, send, recv):
        def copy(step):
            return pltpu.make_async_remote_copy(
                src_ref=src_ref,
                dst_ref=dst_ref.at[d],
                send_sem=send.at[step],
                recv_sem=recv.at[step],
                device_id=(lax.rem(d + step, dp_size), e),
                device_id_type=MESH,
            )

        return copy

    score_copy = row_copy(scores_ref, scores_all, ssend, srecv)
    token_copy = row_copy(tokens_ref, tokens_all, tsend, trecv)
    start_all(score_copy, dp_size)
    start_all(token_copy, dp_size)
    wait_all(score_copy, dp_size)
    per_row = tok_rows // 128
    for step in range(dp_size):
        scores_flat[step * per_row : (step + 1) * per_row, :] = scores_all[step]
    select(capacity, tok_rows, d, scores_flat[...], table_own)
    tables_ref[e] = table_own[...]
    table_copy = expert_copy(exp_size, lambda peer: table_own, tables_ref, send_sems, recv_sems)
    start_all(table_copy, exp_size)
    wait_all(token_copy, dp_size)
    wait_all(table_copy, exp_size)
    turn_tables(exp_size, tables_ref, flat, turned)
    spread(exp_size, slots, turned, token_of)
    picked[...] = jnp.zeros_like(picked)

    @pl.loop(0, dp_size)
    def _(step):
        rows = tokens_all[step]
        rows = jnp.concatenate([rows, jnp.zeros_like(rows)], axis=0)
        picked[...] += lax.dot_general(
            one_hot(token_of, step * tok_rows, tok_rows),
            rows,
            (((1,), (1,)), ((), ())),
            preferred_element_type=jnp.float32,
        )

    half = slots // 2
    for expert in range(exp_size):
        low = picked[expert * slots : expert * slots + half, :]
        high = picked[expert * slots + half : (expert + 1) * slots, :]
        packed[expert] = (low + pltpu.roll(high, 64, 1)).astype(jnp.bfloat16)
    swap = expert_copy(exp_size, lambda peer: packed.at[peer], landed, send_sems2, recv_sems2)
    start_all(swap, exp_size)
    landed[e] = packed[e]
    wait_all(swap, exp_size)
    left = lax.broadcasted_iota(jnp.int32, (half, 128), 1) < 64
    for pair in range(exp_size // 2):
        a = landed[2 * pair].astype(jnp.float32)
        b = landed[2 * pair + 1].astype(jnp.float32)
        cols = pl.ds(pair * 128, 128)
        x_own[0:half, cols] = jnp.where(left, a, pltpu.roll(b, 64, 1)).astype(jnp.bfloat16)
        x_own[half : 2 * half, cols] = jnp.where(left, pltpu.roll(a, 64, 1), b).astype(jnp.bfloat16)

    def across(step):
        return pltpu.make_async_remote_copy(
            src_ref=x_own,
            dst_ref=out_ref.at[d],
            send_sem=dsend.at[step],
            recv_sem=drecv.at[step],
            device_id=(lax.rem(chip + step, chips) * 2 + core, e),
            device_id_type=MESH,
        )

    def beside(step):
        source = lax.rem(chip - step + chips, chips) * 2 + core
        return pltpu.make_async_remote_copy(
            src_ref=x_own if step == 0 else out_ref.at[source],
            dst_ref=out_ref.at[source],
            send_sem=dsend.at[chips + step],
            recv_sem=drecv.at[chips + step],
            device_id=(chip * 2 + 1 - core, e),
            device_id_type=MESH,
        )

    for step in range(1, chips):
        across(step).start()
    beside(0).start()
    out_ref[d] = x_own[...]
    for step in range(1, chips):
        across(step).wait_recv()
        beside(step).start()
    for step in range(1, chips):
        across(step).wait_send()
    for step in range(chips):
        beside(step).wait()


def return_kernel(
    capacity,
    dp_size,
    exp_size,
    x_ref,
    gate_ref,
    up_ref,
    down_ref,
    tables_ref,
    out_ref,
    part,
    from_core,
    pair_sum,
    from_chip,
    packed,
    landed,
    flat,
    turned,
    token_of,
    hits,
    terms,
    terms_turned,
    outgoing,
    outgoing_den,
    incoming,
    incoming_den,
    send_sems,
    recv_sems,
    dsend,
    drecv,
    fsend,
    frecv,
    gsend,
    grecv,
):
    d, e = lax.axis_index("dp"), lax.axis_index("expert")
    chip, core = lax.div(d, 2), lax.rem(d, 2)
    chips = dp_size // 2
    slots = capacity // dp_size
    tok_rows = out_ref.shape[1]
    width = x_ref.shape[1]
    hail(dp_size, exp_size)
    gate_val = project_rows(x_ref[...], gate_ref[...])
    up_val = project_rows(x_ref[...], up_ref[...])
    hidden = (gate_val / (1.0 + jnp.exp(-gate_val)) * up_val).astype(jnp.bfloat16)
    for step in range(width // 512):
        cols = pl.ds(step * 512, 512)
        product = jnp.dot(hidden, down_ref[:, cols], preferred_element_type=jnp.float32)
        part[:, :, cols] = product.astype(jnp.bfloat16).reshape(dp_size, slots, 512)
    meet(dp_size, exp_size)

    def beside(step):
        target = lax.rem(chip + step, chips)
        return pltpu.make_async_remote_copy(
            src_ref=part.at[target * 2 + 1 - core],
            dst_ref=from_core.at[step],
            send_sem=dsend.at[chips + step],
            recv_sem=drecv.at[chips + step],
            device_id=(chip * 2 + 1 - core, e),
            device_id_type=MESH,
        )

    def across(step):
        return pltpu.make_async_remote_copy(
            src_ref=pair_sum.at[step],
            dst_ref=from_chip.at[step],
            send_sem=dsend.at[step],
            recv_sem=drecv.at[step],
            device_id=(lax.rem(chip + step, chips) * 2 + core, e),
            device_id_type=MESH,
        )

    order = [2, 1, 3, 0]
    for step in order:
        beside(step).start()
    for step in order[:-1]:
        beside(step).wait_recv()
        mine = part[lax.rem(chip + step, chips) * 2 + core].astype(jnp.float32)
        pair_sum[step] = (mine + from_core[step].astype(jnp.float32)).astype(jnp.bfloat16)
        across(step).start()
    turn_tables(exp_size, tables_ref, flat, turned)
    spread(exp_size, slots, turned, token_of)
    beside(0).wait_recv()
    for step in order[:-1]:
        across(step).wait_recv()
    half = packed.shape[1]
    left = lax.broadcasted_iota(jnp.int32, (half, 128), 1) < 64
    for pair in range(exp_size // 2):
        cols = pl.ds(pair * 128, 128)
        total = part[d, :, cols].astype(jnp.float32) + from_core[0, :, cols].astype(jnp.float32)
        for step in range(1, chips):
            total += from_chip[step, :, cols].astype(jnp.float32)
        a, b = total[0:half], total[half : 2 * half]
        packed[2 * pair] = jnp.where(left, a, pltpu.roll(b, 64, 1)).astype(jnp.bfloat16)
        packed[2 * pair + 1] = jnp.where(left, pltpu.roll(a, 64, 1), b).astype(jnp.bfloat16)
    swap = expert_copy(exp_size, lambda peer: packed.at[peer], landed, send_sems, recv_sems)
    start_all(swap, exp_size)
    landed[e] = packed[e]
    for step in order[:-1]:
        across(step).wait_send()
    for step in order:
        beside(step).wait_send()

    @pl.loop(0, dp_size)
    def _(step):
        hits[step] = one_hot(token_of, step * tok_rows, tok_rows)

    wait_all(swap, exp_size)
    lane = lax.broadcasted_iota(jnp.int32, (slots, 128), 1)
    for expert in range(exp_size):
        both = landed[expert].astype(jnp.float32)
        value = jnp.concatenate([both, pltpu.roll(both, 64, 1)], axis=0)
        column = turned[0:slots, 2 * expert + 1 : 2 * expert + 2]
        weight = jnp.exp(jnp.broadcast_to(column, (slots, 128)) * SCORE_STEP)
        value = jnp.where(lane < 64, value * weight, 0.0)
        high = value.astype(jnp.bfloat16).astype(jnp.float32)
        rows = pl.ds(expert * slots, slots)
        terms[rows, 0:128] = high + pltpu.roll(value - high, 64, 1)
        first = weight.astype(jnp.bfloat16).astype(jnp.float32)
        second = (weight - first).astype(jnp.bfloat16).astype(jnp.float32)
        third = weight - first - second
        split = jnp.where(lane == 0, first, jnp.where(lane == 1, second, third))
        terms[rows, 128:256] = jnp.where(lane < 3, split, 0.0)
    terms_turned[...] = jnp.transpose(terms[...]).astype(jnp.bfloat16)

    def sum_copy(step):
        return pltpu.make_async_remote_copy(
            src_ref=outgoing.at[step],
            dst_ref=incoming.at[step],
            send_sem=fsend.at[step],
            recv_sem=frecv.at[step],
            device_id=(lax.rem(d + step, dp_size), e),
            device_id_type=MESH,
        )

    def den_copy(step):
        return pltpu.make_async_remote_copy(
            src_ref=outgoing_den.at[step],
            dst_ref=incoming_den.at[step],
            send_sem=gsend.at[step],
            recv_sem=grecv.at[step],
            device_id=(lax.rem(d + step, dp_size), e),
            device_id_type=MESH,
        )

    def row_sums(step):
        sums = jnp.dot(
            terms_turned[...], hits[lax.rem(d + step, dp_size)], preferred_element_type=jnp.float32
        )
        return sums[0:64] + sums[64:128], jnp.sum(sums[128:136], axis=0, keepdims=True)

    @pl.loop(1, dp_size)
    def _(step):
        sums, den = row_sums(step)
        outgoing[step] = sums.astype(jnp.bfloat16)
        outgoing_den[step] = den
        sum_copy(step).start()
        den_copy(step).start()

    total, den = row_sums(0)
    wait_all(sum_copy, dp_size)
    wait_all(den_copy, dp_size)
    for step in range(1, dp_size):
        total += incoming[step].astype(jnp.float32)
        den += incoming_den[step]
    out_ref[...] = (total / jnp.maximum(den, 1.0)).astype(jnp.bfloat16)


def project_rows(inputs, weight_rows):
    return lax.dot_general(
        inputs, weight_rows, (((1,), (1,)), ((), ())), preferred_element_type=jnp.float32
    )


def local(capacity, dp_size, exp_size, scores, tokens, w_gate, w_up, w_down):
    tok_rows, block = tokens.shape
    width = block * exp_size
    slots = capacity // dp_size
    half = slots // 2
    chips = dp_size // 2
    dma = pltpu.SemaphoreType.DMA
    bf16, f32, i32 = jnp.bfloat16, jnp.float32, jnp.int32
    all_rows = tok_rows * dp_size // 128
    inputs, tables = pl.pallas_call(
        functools.partial(dispatch_kernel, capacity, dp_size, exp_size),
        out_shape=(
            jax.ShapeDtypeStruct((dp_size, slots, width), bf16),
            jax.ShapeDtypeStruct((exp_size, 2, 128), i32),
        ),
        in_specs=[VMEM] * 2,
        out_specs=(VMEM, VMEM),
        scratch_shapes=[
            pltpu.VMEM((dp_size, tok_rows // 128, 128), i32),
            pltpu.VMEM((all_rows, 128), i32),
            pltpu.VMEM((dp_size, block, tok_rows), bf16),
            pltpu.VMEM((2, 128), i32),
            pltpu.VMEM((2 * exp_size, 128), f32),
            pltpu.VMEM((128, 2 * exp_size), f32),
            pltpu.VMEM((exp_size * slots, 128), i32),
            pltpu.VMEM((exp_size * slots, 128), f32),
            pltpu.VMEM((exp_size, half, 128), bf16),
            pltpu.VMEM((exp_size, half, 128), bf16),
            pltpu.VMEM((slots, width), bf16),
            dma((dp_size,)),
            dma((dp_size,)),
            dma((dp_size,)),
            dma((dp_size,)),
            dma((exp_size,)),
            dma((exp_size,)),
            dma((exp_size,)),
            dma((exp_size,)),
            dma((dp_size,)),
            dma((dp_size,)),
        ],
        compiler_params=params(0),
    )(scores.reshape(tok_rows // 128, 128), tokens.T)
    mixed = pl.pallas_call(
        functools.partial(return_kernel, capacity, dp_size, exp_size),
        out_shape=jax.ShapeDtypeStruct((block, tok_rows), bf16),
        in_specs=[VMEM] * 5,
        out_specs=VMEM,
        scratch_shapes=[
            pltpu.VMEM((dp_size, slots, width), bf16),
            pltpu.VMEM((chips, slots, width), bf16),
            pltpu.VMEM((chips, slots, width), bf16),
            pltpu.VMEM((chips, slots, width), bf16),
            pltpu.VMEM((exp_size, half, 128), bf16),
            pltpu.VMEM((exp_size, half, 128), bf16),
            pltpu.VMEM((2 * exp_size, 128), f32),
            pltpu.VMEM((128, 2 * exp_size), f32),
            pltpu.VMEM((exp_size * slots, 128), i32),
            pltpu.VMEM((dp_size, exp_size * slots, tok_rows), bf16),
            pltpu.VMEM((exp_size * slots, 256), f32),
            pltpu.VMEM((256, exp_size * slots), bf16),
            pltpu.VMEM((dp_size, block, tok_rows), bf16),
            pltpu.VMEM((dp_size, 1, tok_rows), f32),
            pltpu.VMEM((dp_size, block, tok_rows), bf16),
            pltpu.VMEM((dp_size, 1, tok_rows), f32),
            dma((exp_size,)),
            dma((exp_size,)),
            dma((dp_size,)),
            dma((dp_size,)),
            dma((dp_size,)),
            dma((dp_size,)),
            dma((dp_size,)),
            dma((dp_size,)),
        ],
        compiler_params=params(1),
    )(inputs.reshape(capacity, width), w_gate[0], w_up[0], w_down[0], tables)
    return mixed.T


def solution(mesh):
    dp_size, exp_size = mesh.shape["dp"], mesh.shape["expert"]
    in_specs = (
        P("expert", "dp"),
        P("dp", "expert"),
        P("expert", "dp", None),
        P("expert", "dp", None),
        P("expert", "dp", None),
    )

    def layer(scores, tokens, w_gate, w_up, w_down):
        capacity = 4 * scores.shape[1] // exp_size
        return jax.shard_map(
            functools.partial(local, capacity, dp_size, exp_size),
            mesh=mesh,
            in_specs=in_specs,
            out_specs=P("dp", "expert"),
            check_vma=False,
        )(scores, tokens, w_gate, w_up, w_down)

    return layer
```

time: 197 us -> 138 us (0.70)
  blocking collectives: 35.8 us -> 0 us
  local copies, waits for them, and re-layouts: 16.6 us -> 1.47 us
  other arithmetic: 14.9 us -> 0 us
  Pallas kernels: 123 us -> 136 us
  matrix products: 6.29 us -> 0 us
    all_gather x2 -> x0, blocking collectives: 35.8 us -> none  [the longest x1 18.9 us: local(): lax.all_gather(scores[0], 'dp', axis=0, tiled=True).reshape(-1, 128)]
    scatter-add x1 -> x0, other arithmetic: 13.9 us -> none  [local(): sums = jnp.zeros((all_tokens, block), jnp.float32).at[slot_tokens.reshape...]
    pallas_call x5 -> x2, Pallas kernels: 123 us -> 136 us  [the longest x1 79.3 us: local(): pl.pallas_call(functools.partial(dispatch_kernel, capacity, dp_size, exp_...]
    gather x2 -> x0, local copies, waits for them, and re-layouts: 6.41 us -> none  [the longest x1 3.21 us: local(): gathered[slot_tokens[:, :half]]]
    dot_general x2 -> x0, matrix products: 6.29 us -> none  [the longest x1 5.44 us: local(): jnp.dot(hidden, w_down[0], preferred_element_type=jnp.float32)]
    unnamed x15 -> x1, local copies, waits for them, and re-layouts: 5.62 us -> 1.47 us
where the time goes in v2:
time: 138 us; the launch traced here: 137 us
  Pallas kernels  136 us (99%)
  local copies, waits for them, and re-layouts  1.47 us (1%)
    pallas_call x1, Pallas kernels, local(): pl.pallas_call(functools.partial(dispatch_kernel, capacity, dp_size, exp_...  79.3 us
    pallas_call x1, Pallas kernels, local(): pl.pallas_call(functools.partial(return_kernel, capacity, dp_size, exp_si...  56.6 us

profile of v2, /device:TPU:1, one launch (start us, length us, event | category | flops | bytes accessed | tf_op | source)
XLA Modules:
  0.0 137.5 jit_solution(2155876883244739512)
XLA Ops:
  0.0 79.3 %shard_map.55 = (bf16[8,32,4096]{2,1,0:T(8,128)(2,1)}, s32[64,2,128]{2,1,0:T(2,128)}) custom-call(s32[4,128]{1,0:T(4,128)} %bitcast.13, bf16[64,512]{1,0:T(8,128)(2,1)} %bitcast.12), custom_call_target="tpu_custom_call" | custom-call | tf_op jit(solution)/shard_map/pallas_call | solution.py:458
  79.3 56.6 %shard_map.56 = bf16[64,512]{1,0:T(8,128)(2,1)} custom-call(bf16[256,4096]{1,0:T(8,128)(2,1)} %bitcast.7, bf16[192,4096]{1,0:T(8,128)(2,1)} %bitcast.8, bf16[192,4096]{1,0:T(8,128)(2,1)} %bitcast.9, bf16[192,4096]{1,0:T(8,128)(2,1)} %bitcast.10, s32[64,2,128]{2,1,0:T(2,128)} %get-tuple-element.8.tables_ref), custom_call_target="tpu_custom_call" | custom-call | tf_op jit(solution)/shard_map/pallas_call | solution.py:491
  136.0 1.5 %copy.7 = bf16[512,64]{0,1:T(8,128)(2,1)} copy(bf16[512,64]{0,1:T(8,128)(2,1)} %bitcast.11) | data formatting | bytes 131072

commit v3 on v2

--- a/solution.py
+++ b/solution.py
@@ -19,20 +19,25 @@
     )
 
 
+def far_first(index, size):
+    rank = size - index
+    near, odd = lax.div(rank + 1, 2), lax.rem(rank, 2)
+    return odd * near + (1 - odd) * (size - near)
+
+
 def hail(dp_size, exp_size):
     d, e = lax.axis_index("dp"), lax.axis_index("expert")
     barrier = pltpu.get_barrier_semaphore()
+
+    @pl.loop(1, exp_size)
+    def _(index):
+        peer = lax.rem(e + far_first(index, exp_size), exp_size)
+        pl.semaphore_signal(barrier, inc=1, device_id=(d, peer), device_id_type=MESH)
 
     @pl.loop(1, dp_size)
     def _(step):
         pl.semaphore_signal(
             barrier, inc=1, device_id=(lax.rem(d + step, dp_size), e), device_id_type=MESH
-        )
-
-    @pl.loop(1, exp_size)
-    def _(step):
-        pl.semaphore_signal(
-            barrier, inc=1, device_id=(d, lax.rem(e + step, exp_size)), device_id_type=MESH
         )
 
 
@@ -110,16 +115,17 @@
     return jnp.concatenate(parts, axis=1)
 
 
-def expert_copy(exp_size, src_of, dst_ref, send_sems, recv_sems):
+def expert_copy(exp_size, src_of, dst_ref, send_sems, recv_sems, first=0):
     d, e = lax.axis_index("dp"), lax.axis_index("expert")
 
-    def copy(step):
+    def copy(index):
+        step = far_first(index, exp_size)
         peer = lax.rem(e + step, exp_size)
         return pltpu.make_async_remote_copy(
             src_ref=src_of(peer),
             dst_ref=dst_ref.at[e],
-            send_sem=send_sems.at[step],
-            recv_sem=recv_sems.at[step],
+            send_sem=send_sems.at[first + step],
+            recv_sem=recv_sems.at[first + step],
             device_id=(d, peer),
             device_id_type=MESH,
         )
@@ -221,55 +227,70 @@
             preferred_element_type=jnp.float32,
         )
 
-    half = slots // 2
-    for expert in range(exp_size):
-        low = picked[expert * slots : expert * slots + half, :]
-        high = picked[expert * slots + half : (expert + 1) * slots, :]
-        packed[expert] = (low + pltpu.roll(high, 64, 1)).astype(jnp.bfloat16)
-    swap = expert_copy(exp_size, lambda peer: packed.at[peer], landed, send_sems2, recv_sems2)
-    start_all(swap, exp_size)
-    landed[e] = packed[e]
-    wait_all(swap, exp_size)
-    left = lax.broadcasted_iota(jnp.int32, (half, 128), 1) < 64
-    for pair in range(exp_size // 2):
-        a = landed[2 * pair].astype(jnp.float32)
-        b = landed[2 * pair + 1].astype(jnp.float32)
-        cols = pl.ds(pair * 128, 128)
-        x_own[0:half, cols] = jnp.where(left, a, pltpu.roll(b, 64, 1)).astype(jnp.bfloat16)
-        x_own[half : 2 * half, cols] = jnp.where(left, pltpu.roll(a, 64, 1), b).astype(jnp.bfloat16)
-
-    def across(step):
-        return pltpu.make_async_remote_copy(
-            src_ref=x_own,
-            dst_ref=out_ref.at[d],
-            send_sem=dsend.at[step],
-            recv_sem=drecv.at[step],
+    quarter = slots // 4
+    swaps = []
+    for half in range(2):
+        for expert in range(exp_size):
+            row = expert * slots + half * 2 * quarter
+            low = picked[row : row + quarter, :]
+            high = picked[row + quarter : row + 2 * quarter, :]
+            packed[half, expert] = (low + pltpu.roll(high, 64, 1)).astype(jnp.bfloat16)
+        swap = expert_copy(
+            exp_size,
+            lambda peer, half=half: packed.at[half, peer],
+            landed.at[half],
+            send_sems2,
+            recv_sems2,
+            half * exp_size,
+        )
+        start_all(swap, exp_size)
+        landed[half, e] = packed[half, e]
+        swaps.append(swap)
+
+    def across(half, step):
+        return pltpu.make_async_remote_copy(
+            src_ref=x_own.at[half],
+            dst_ref=out_ref.at[d, half],
+            send_sem=dsend.at[half * dp_size + step],
+            recv_sem=drecv.at[half * dp_size + step],
             device_id=(lax.rem(chip + step, chips) * 2 + core, e),
             device_id_type=MESH,
         )
 
-    def beside(step):
+    def beside(half, step):
         source = lax.rem(chip - step + chips, chips) * 2 + core
         return pltpu.make_async_remote_copy(
-            src_ref=x_own if step == 0 else out_ref.at[source],
-            dst_ref=out_ref.at[source],
-            send_sem=dsend.at[chips + step],
-            recv_sem=drecv.at[chips + step],
+            src_ref=x_own.at[half] if step == 0 else out_ref.at[source, half],
+            dst_ref=out_ref.at[source, half],
+            send_sem=dsend.at[half * dp_size + chips + step],
+            recv_sem=drecv.at[half * dp_size + chips + step],
             device_id=(chip * 2 + 1 - core, e),
             device_id_type=MESH,
         )
 
-    for step in range(1, chips):
-        across(step).start()
-    beside(0).start()
-    out_ref[d] = x_own[...]
-    for step in range(1, chips):
-        across(step).wait_recv()
-        beside(step).start()
-    for step in range(1, chips):
-        across(step).wait_send()
-    for step in range(chips):
-        beside(step).wait()
+    left = lax.broadcasted_iota(jnp.int32, (quarter, 128), 1) < 64
+    for half in range(2):
+        wait_all(swaps[half], exp_size)
+        for pair in range(exp_size // 2):
+            a = landed[half, 2 * pair].astype(jnp.float32)
+            b = landed[half, 2 * pair + 1].astype(jnp.float32)
+            first = jnp.where(left, a, pltpu.roll(b, 64, 1))
+            second = jnp.where(left, pltpu.roll(a, 64, 1), b)
+            rows = jnp.concatenate([first, second], axis=0).astype(jnp.bfloat16)
+            x_own[half, :, pl.ds(pair * 128, 128)] = rows
+        for step in range(1, chips):
+            across(half, step).start()
+        beside(half, 0).start()
+        out_ref[d, half] = x_own[half]
+    for half in range(2):
+        for step in range(1, chips):
+            across(half, step).wait_recv()
+            beside(half, step).start()
+    for half in range(2):
+        for step in range(1, chips):
+            across(half, step).wait_send()
+        for step in range(chips):
+            beside(half, step).wait()
 
 
 def return_kernel(
@@ -320,70 +341,91 @@
     for step in range(width // 512):
         cols = pl.ds(step * 512, 512)
         product = jnp.dot(hidden, down_ref[:, cols], preferred_element_type=jnp.float32)
-        part[:, :, cols] = product.astype(jnp.bfloat16).reshape(dp_size, slots, 512)
+        part[:, :, :, cols] = product.astype(jnp.bfloat16).reshape(dp_size, 2, slots // 2, 512)
     meet(dp_size, exp_size)
 
-    def beside(step):
+    def beside(half, step):
         target = lax.rem(chip + step, chips)
         return pltpu.make_async_remote_copy(
-            src_ref=part.at[target * 2 + 1 - core],
-            dst_ref=from_core.at[step],
-            send_sem=dsend.at[chips + step],
-            recv_sem=drecv.at[chips + step],
+            src_ref=part.at[target * 2 + 1 - core, half],
+            dst_ref=from_core.at[half, step],
+            send_sem=dsend.at[half * dp_size + chips + step],
+            recv_sem=drecv.at[half * dp_size + chips + step],
             device_id=(chip * 2 + 1 - core, e),
             device_id_type=MESH,
         )
 
-    def across(step):
-        return pltpu.make_async_remote_copy(
-            src_ref=pair_sum.at[step],
-            dst_ref=from_chip.at[step],
-            send_sem=dsend.at[step],
-            recv_sem=drecv.at[step],
+    def across(half, step):
+        return pltpu.make_async_remote_copy(
+            src_ref=pair_sum.at[half, step],
+            dst_ref=from_chip.at[half, step],
+            send_sem=dsend.at[half * dp_size + step],
+            recv_sem=drecv.at[half * dp_size + step],
             device_id=(lax.rem(chip + step, chips) * 2 + core, e),
             device_id_type=MESH,
         )
 
     order = [2, 1, 3, 0]
-    for step in order:
-        beside(step).start()
-    for step in order[:-1]:
-        beside(step).wait_recv()
-        mine = part[lax.rem(chip + step, chips) * 2 + core].astype(jnp.float32)
-        pair_sum[step] = (mine + from_core[step].astype(jnp.float32)).astype(jnp.bfloat16)
-        across(step).start()
+    for half in range(2):
+        for step in order:
+            beside(half, step).start()
+    for half in range(2):
+        for step in order[:-1]:
+            beside(half, step).wait_recv()
+            mine = part[lax.rem(chip + step, chips) * 2 + core, half].astype(jnp.float32)
+            mine += from_core[half, step].astype(jnp.float32)
+            pair_sum[half, step] = mine.astype(jnp.bfloat16)
+            across(half, step).start()
     turn_tables(exp_size, tables_ref, flat, turned)
     spread(exp_size, slots, turned, token_of)
-    beside(0).wait_recv()
-    for step in order[:-1]:
-        across(step).wait_recv()
-    half = packed.shape[1]
-    left = lax.broadcasted_iota(jnp.int32, (half, 128), 1) < 64
-    for pair in range(exp_size // 2):
-        cols = pl.ds(pair * 128, 128)
-        total = part[d, :, cols].astype(jnp.float32) + from_core[0, :, cols].astype(jnp.float32)
-        for step in range(1, chips):
-            total += from_chip[step, :, cols].astype(jnp.float32)
-        a, b = total[0:half], total[half : 2 * half]
-        packed[2 * pair] = jnp.where(left, a, pltpu.roll(b, 64, 1)).astype(jnp.bfloat16)
-        packed[2 * pair + 1] = jnp.where(left, pltpu.roll(a, 64, 1), b).astype(jnp.bfloat16)
-    swap = expert_copy(exp_size, lambda peer: packed.at[peer], landed, send_sems, recv_sems)
-    start_all(swap, exp_size)
-    landed[e] = packed[e]
-    for step in order[:-1]:
-        across(step).wait_send()
-    for step in order:
-        beside(step).wait_send()
+    quarter = slots // 4
+    left = lax.broadcasted_iota(jnp.int32, (quarter, 128), 1) < 64
+    swaps = []
+    for half in range(2):
+        beside(half, 0).wait_recv()
+        for step in order[:-1]:
+            across(half, step).wait_recv()
+        for pair in range(exp_size // 2):
+            cols = pl.ds(pair * 128, 128)
+            total = part[d, half, :, cols].astype(jnp.float32)
+            total += from_core[half, 0, :, cols].astype(jnp.float32)
+            for step in range(1, chips):
+                total += from_chip[half, step, :, cols].astype(jnp.float32)
+            a, b = total[0:quarter], total[quarter : 2 * quarter]
+            first = jnp.where(left, a, pltpu.roll(b, 64, 1))
+            second = jnp.where(left, pltpu.roll(a, 64, 1), b)
+            packed[half, 2 * pair] = first.astype(jnp.bfloat16)
+            packed[half, 2 * pair + 1] = second.astype(jnp.bfloat16)
+        swap = expert_copy(
+            exp_size,
+            lambda peer, half=half: packed.at[half, peer],
+            landed.at[half],
+            send_sems,
+            recv_sems,
+            half * exp_size,
+        )
+        start_all(swap, exp_size)
+        landed[half, e] = packed[half, e]
+        swaps.append(swap)
+    for half in range(2):
+        for step in order[:-1]:
+            across(half, step).wait_send()
+        for step in order:
+            beside(half, step).wait_send()
 
     @pl.loop(0, dp_size)
     def _(step):
         hits[step] = one_hot(token_of, step * tok_rows, tok_rows)
 
-    wait_all(swap, exp_size)
+    for swap in swaps:
+        wait_all(swap, exp_size)
     lane = lax.broadcasted_iota(jnp.int32, (slots, 128), 1)
     for expert in range(exp_size):
-        both = landed[expert].astype(jnp.float32)
-        value = jnp.concatenate([both, pltpu.roll(both, 64, 1)], axis=0)
+        value = []
+        for half in range(2):
+            both = landed[half, expert].astype(jnp.float32)
+            value += [both, pltpu.roll(both, 64, 1)]
+        value = jnp.concatenate(value, axis=0)
         column = turned[0:slots, 2 * expert + 1 : 2 * expert + 2]
         weight = jnp.exp(jnp.broadcast_to(column, (slots, 128)) * SCORE_STEP)
         value = jnp.where(lane < 64, value * weight, 0.0)
@@ -458,7 +500,7 @@
     inputs, tables = pl.pallas_call(
         functools.partial(dispatch_kernel, capacity, dp_size, exp_size),
         out_shape=(
-            jax.ShapeDtypeStruct((dp_size, slots, width), bf16),
+            jax.ShapeDtypeStruct((dp_size, 2, half, width), bf16),
             jax.ShapeDtypeStruct((exp_size, 2, 128), i32),
         ),
         in_specs=[VMEM] * 2,
@@ -472,19 +514,19 @@
             pltpu.VMEM((128, 2 * exp_size), f32),
             pltpu.VMEM((exp_size * slots, 128), i32),
             pltpu.VMEM((exp_size * slots, 128), f32),
-            pltpu.VMEM((exp_size, half, 128), bf16),
-            pltpu.VMEM((exp_size, half, 128), bf16),
-            pltpu.VMEM((slots, width), bf16),
+            pltpu.VMEM((2, exp_size, half // 2, 128), bf16),
+            pltpu.VMEM((2, exp_size, half // 2, 128), bf16),
+            pltpu.VMEM((2, half, width), bf16),
             dma((dp_size,)),
             dma((dp_size,)),
             dma((dp_size,)),
             dma((dp_size,)),
             dma((exp_size,)),
             dma((exp_size,)),
-            dma((exp_size,)),
-            dma((exp_size,)),
-            dma((dp_size,)),
-            dma((dp_size,)),
+            dma((2 * exp_size,)),
+            dma((2 * exp_size,)),
+            dma((2 * dp_size,)),
+            dma((2 * dp_size,)),
         ],
         compiler_params=params(0),
     )(scores.reshape(tok_rows // 128, 128), tokens.T)
@@ -494,12 +536,12 @@
         in_specs=[VMEM] * 5,
         out_specs=VMEM,
         scratch_shapes=[
-            pltpu.VMEM((dp_size, slots, width), bf16),
-            pltpu.VMEM((chips, slots, width), bf16),
-            pltpu.VMEM((chips, slots, width), bf16),
-            pltpu.VMEM((chips, slots, width), bf16),
-            pltpu.VMEM((exp_size, half, 128), bf16),
-            pltpu.VMEM((exp_size, half, 128), bf16),
+            pltpu.VMEM((dp_size, 2, half, width), bf16),
+            pltpu.VMEM((2, chips, half, width), bf16),
+            pltpu.VMEM((2, chips, half, width), bf16),
+            pltpu.VMEM((2, chips, half, width), bf16),
+            pltpu.VMEM((2, exp_size, half // 2, 128), bf16),
+            pltpu.VMEM((2, exp_size, half // 2, 128), bf16),
             pltpu.VMEM((2 * exp_size, 128), f32),
             pltpu.VMEM((128, 2 * exp_size), f32),
             pltpu.VMEM((exp_size * slots, 128), i32),
@@ -510,10 +552,10 @@
             pltpu.VMEM((dp_size, 1, tok_rows), f32),
             pltpu.VMEM((dp_size, block, tok_rows), bf16),
             pltpu.VMEM((dp_size, 1, tok_rows), f32),
-            dma((exp_size,)),
-            dma((exp_size,)),
-            dma((dp_size,)),
-            dma((dp_size,)),
+            dma((2 * exp_size,)),
+            dma((2 * exp_size,)),
+            dma((2 * dp_size,)),
+            dma((2 * dp_size,)),
             dma((dp_size,)),
             dma((dp_size,)),
             dma((dp_size,)),

time: 138 us -> 125 us (0.906)
  Pallas kernels: 136 us -> 124 us
    pallas_call x1, Pallas kernels: 79.3 us -> 71 us  [local(): pl.pallas_call(functools.partial(dispatch_kernel, capacity, dp_size, exp_...]
    pallas_call x1, Pallas kernels: 56.6 us -> 52.8 us  [local(): pl.pallas_call(functools.partial(return_kernel, capacity, dp_size, exp_si...]
where the time goes in v3:
time: 125 us
  Pallas kernels  124 us (99%)
  local copies, waits for them, and re-layouts  1.47 us (1%)
    pallas_call x1, Pallas kernels, local(): pl.pallas_call(functools.partial(dispatch_kernel, capacity, dp_size, exp_...  71 us
    pallas_call x1, Pallas kernels, local(): pl.pallas_call(functools.partial(return_kernel, capacity, dp_size, exp_si...  52.8 us

profile of v3, /device:TPU:1, one launch (start us, length us, event | category | flops | bytes accessed | tf_op | source)
XLA Modules:
  0.0 125.2 jit_solution(12440934940406741680)
XLA Ops:
  0.0 71.0 %shard_map.55 = (bf16[8,2,16,4096]{3,2,1,0:T(8,128)(2,1)}, s32[64,2,128]{2,1,0:T(2,128)}) custom-call(s32[4,128]{1,0:T(4,128)} %bitcast.13, bf16[64,512]{1,0:T(8,128)(2,1)} %bitcast.12), custom_call_target="tpu_custom_call" | custom-call | tf_op jit(solution)/shard_map/pallas_call | solution.py:500
  71.0 52.8 %shard_map.56 = bf16[64,512]{1,0:T(8,128)(2,1)} custom-call(bf16[256,4096]{1,0:T(8,128)(2,1)} %bitcast.7, bf16[192,4096]{1,0:T(8,128)(2,1)} %bitcast.8, bf16[192,4096]{1,0:T(8,128)(2,1)} %bitcast.9, bf16[192,4096]{1,0:T(8,128)(2,1)} %bitcast.10, s32[64,2,128]{2,1,0:T(2,128)} %get-tuple-element.8.tables_ref), custom_call_target="tpu_custom_call" | custom-call | tf_op jit(solution)/shard_map/pallas_call | solution.py:533
  123.7 1.5 %copy.7 = bf16[512,64]{0,1:T(8,128)(2,1)} copy(bf16[512,64]{0,1:T(8,128)(2,1)} %bitcast.11) | data formatting | bytes 131072

commit v4 on v3

--- a/solution.py
+++ b/solution.py
@@ -102,12 +102,15 @@
 def spread(exp_size, slots, turned, token_of):
     for expert in range(exp_size):
         column = turned[0:slots, 2 * expert : 2 * expert + 1].astype(jnp.int32)
-        token_of[expert * slots : (expert + 1) * slots, :] = jnp.broadcast_to(column, (slots, 128))
+        column = jnp.broadcast_to(column, (slots, 128))
+        for half in range(2):
+            row = (half * exp_size + expert) * (slots // 2)
+            token_of[row : row + slots // 2, :] = column[half * slots // 2 : (half + 1) * slots // 2]
 
 
 def one_hot(token_of, first, tok_rows):
     lane = lax.broadcasted_iota(jnp.int32, token_of.shape, 1)
-    own = token_of[...] - first
+    own = token_of - first
     parts = [
         jnp.where(own == lane + step * 128, 1.0, 0.0).astype(jnp.bfloat16)
         for step in range(tok_rows // 128)
@@ -214,24 +217,25 @@
     wait_all(table_copy, exp_size)
     turn_tables(exp_size, tables_ref, flat, turned)
     spread(exp_size, slots, turned, token_of)
-    picked[...] = jnp.zeros_like(picked)
-
-    @pl.loop(0, dp_size)
-    def _(step):
-        rows = tokens_all[step]
-        rows = jnp.concatenate([rows, jnp.zeros_like(rows)], axis=0)
-        picked[...] += lax.dot_general(
-            one_hot(token_of, step * tok_rows, tok_rows),
-            rows,
-            (((1,), (1,)), ((), ())),
-            preferred_element_type=jnp.float32,
-        )
-
     quarter = slots // 4
     swaps = []
     for half in range(2):
+        picked[...] = jnp.zeros_like(picked)
+        rows_of = pl.ds(half * picked.shape[0], picked.shape[0])
+
+        @pl.loop(0, dp_size)
+        def _(step, rows_of=rows_of):
+            rows = tokens_all[step]
+            rows = jnp.concatenate([rows, jnp.zeros_like(rows)], axis=0)
+            picked[...] += lax.dot_general(
+                one_hot(token_of[rows_of, :], step * tok_rows, tok_rows),
+                rows,
+                (((1,), (1,)), ((), ())),
+                preferred_element_type=jnp.float32,
+            )
+
         for expert in range(exp_size):
-            row = expert * slots + half * 2 * quarter
+            row = expert * 2 * quarter
             low = picked[row : row + quarter, :]
             high = picked[row + quarter : row + 2 * quarter, :]
             packed[half, expert] = (low + pltpu.roll(high, 64, 1)).astype(jnp.bfloat16)
@@ -315,6 +319,7 @@
     hits,
     terms,
     terms_turned,
+    weight_of,
     outgoing,
     outgoing_den,
     incoming,
@@ -415,29 +420,34 @@
 
     @pl.loop(0, dp_size)
     def _(step):
-        hits[step] = one_hot(token_of, step * tok_rows, tok_rows)
-
-    for swap in swaps:
-        wait_all(swap, exp_size)
+        hits[step] = one_hot(token_of[...], step * tok_rows, tok_rows)
+
     lane = lax.broadcasted_iota(jnp.int32, (slots, 128), 1)
     for expert in range(exp_size):
-        value = []
-        for half in range(2):
-            both = landed[half, expert].astype(jnp.float32)
-            value += [both, pltpu.roll(both, 64, 1)]
-        value = jnp.concatenate(value, axis=0)
         column = turned[0:slots, 2 * expert + 1 : 2 * expert + 2]
         weight = jnp.exp(jnp.broadcast_to(column, (slots, 128)) * SCORE_STEP)
-        value = jnp.where(lane < 64, value * weight, 0.0)
-        high = value.astype(jnp.bfloat16).astype(jnp.float32)
-        rows = pl.ds(expert * slots, slots)
-        terms[rows, 0:128] = high + pltpu.roll(value - high, 64, 1)
         first = weight.astype(jnp.bfloat16).astype(jnp.float32)
         second = (weight - first).astype(jnp.bfloat16).astype(jnp.float32)
         third = weight - first - second
         split = jnp.where(lane == 0, first, jnp.where(lane == 1, second, third))
-        terms[rows, 128:256] = jnp.where(lane < 3, split, 0.0)
-    terms_turned[...] = jnp.transpose(terms[...]).astype(jnp.bfloat16)
+        split = jnp.where(lane < 3, split, 0.0)
+        weight = jnp.where(lane < 64, weight, 0.0)
+        for half in range(2):
+            rows = pl.ds((half * exp_size + expert) * 2 * quarter, 2 * quarter)
+            part_rows = slice(half * 2 * quarter, (half + 1) * 2 * quarter)
+            weight_of[rows, :] = weight[part_rows]
+            terms[rows, 128:256] = split[part_rows]
+    count = exp_size * 2 * quarter
+    for half in range(2):
+        wait_all(swaps[half], exp_size)
+        for expert in range(exp_size):
+            rows = pl.ds((half * exp_size + expert) * 2 * quarter, 2 * quarter)
+            both = landed[half, expert].astype(jnp.float32)
+            value = jnp.concatenate([both, pltpu.roll(both, 64, 1)], axis=0) * weight_of[rows, :]
+            high = value.astype(jnp.bfloat16).astype(jnp.float32)
+            terms[rows, 0:128] = high + pltpu.roll(value - high, 64, 1)
+        rows = slice(half * count, (half + 1) * count)
+        terms_turned[:, rows] = jnp.transpose(terms[rows, :]).astype(jnp.bfloat16)
 
     def sum_copy(step):
         return pltpu.make_async_remote_copy(
@@ -513,7 +523,7 @@
             pltpu.VMEM((2 * exp_size, 128), f32),
             pltpu.VMEM((128, 2 * exp_size), f32),
             pltpu.VMEM((exp_size * slots, 128), i32),
-            pltpu.VMEM((exp_size * slots, 128), f32),
+            pltpu.VMEM((exp_size * half, 128), f32),
             pltpu.VMEM((2, exp_size, half // 2, 128), bf16),
             pltpu.VMEM((2, exp_size, half // 2, 128), bf16),
             pltpu.VMEM((2, half, width), bf16),
@@ -548,6 +558,7 @@
             pltpu.VMEM((dp_size, exp_size * slots, tok_rows), bf16),
             pltpu.VMEM((exp_size * slots, 256), f32),
             pltpu.VMEM((256, exp_size * slots), bf16),
+            pltpu.VMEM((exp_size * slots, 128), f32),
             pltpu.VMEM((dp_size, block, tok_rows), bf16),
             pltpu.VMEM((dp_size, 1, tok_rows), f32),
             pltpu.VMEM((dp_size, block, tok_rows), bf16),

time: 125 us -> 118 us (0.944)
  Pallas kernels: 124 us -> 117 us
    pallas_call x1, Pallas kernels: 52.8 us -> 48.5 us  [local(): pl.pallas_call(functools.partial(return_kernel, capacity, dp_size, exp_si...]
    pallas_call x1, Pallas kernels: 71 us -> 68.3 us  [local(): pl.pallas_call(functools.partial(dispatch_kernel, capacity, dp_size, exp_...]
where the time goes in v4:
time: 118 us
  Pallas kernels  117 us (99%)
  local copies, waits for them, and re-layouts  1.47 us (1%)
    pallas_call x1, Pallas kernels, local(): pl.pallas_call(functools.partial(dispatch_kernel, capacity, dp_size, exp_...  68.3 us
    pallas_call x1, Pallas kernels, local(): pl.pallas_call(functools.partial(return_kernel, capacity, dp_size, exp_si...  48.5 us

profile of v4, /device:TPU:1, one launch (start us, length us, event | category | flops | bytes accessed | tf_op | source)
XLA Modules:
  0.0 118.3 jit_solution(13835721548235289139)
XLA Ops:
  0.0 68.3 %shard_map.55 = (bf16[8,2,16,4096]{3,2,1,0:T(8,128)(2,1)}, s32[64,2,128]{2,1,0:T(2,128)}) custom-call(s32[4,128]{1,0:T(4,128)} %bitcast.13, bf16[64,512]{1,0:T(8,128)(2,1)} %bitcast.12), custom_call_target="tpu_custom_call" | custom-call | tf_op jit(solution)/shard_map/pallas_call | solution.py:510
  68.3 48.5 %shard_map.56 = bf16[64,512]{1,0:T(8,128)(2,1)} custom-call(bf16[256,4096]{1,0:T(8,128)(2,1)} %bitcast.7, bf16[192,4096]{1,0:T(8,128)(2,1)} %bitcast.8, bf16[192,4096]{1,0:T(8,128)(2,1)} %bitcast.9, bf16[192,4096]{1,0:T(8,128)(2,1)} %bitcast.10, s32[64,2,128]{2,1,0:T(2,128)} %get-tuple-element.8.tables_ref), custom_call_target="tpu_custom_call" | custom-call | tf_op jit(solution)/shard_map/pallas_call | solution.py:543
  116.8 1.5 %copy.7 = bf16[512,64]{0,1:T(8,128)(2,1)} copy(bf16[512,64]{0,1:T(8,128)(2,1)} %bitcast.11) | data formatting | bytes 131072
